TPU v7x, 32 devices: a whole 2x2x4 slice. The times are simulated.
32 devices in a mesh: dp: 8 (over z, y), expert: 4 (over x, core).
Axes of the slice: x: 2, y: 2, z: 4, core: 2. Of those that a mesh axis runs over, the one named last changes fastest.
Arguments:
- tokens: bfloat16 [512, 2048], P(('dp', 'expert')), may hold values from -6 to 6
- expert_ids: int32 [512, 8], P(('dp', 'expert')), may hold values from 0 to 15, as said below
- route_weight: float32 [512, 8], P(('dp', 'expert')), may hold values from 0.03 to 0.6
- out_grad: bfloat16 [512, 2048], P(('dp', 'expert')), may hold values from -6 to 6
- gate_weight: bfloat16 [32, 2048, 384], P(('dp', 'expert')), may hold values from -0.125 to 0.125
- up_weight: bfloat16 [32, 2048, 384], P(('dp', 'expert')), may hold values from -0.125 to 0.125
- down_weight: bfloat16 [32, 384, 2048], P(('dp', 'expert')), may hold values from -0.21875 to 0.21875
Outputs:
- layer_out: bfloat16 [512, 2048], P(('dp', 'expert'))
- token_grad: bfloat16 [512, 2048], P(('dp', 'expert'))
- route_grad: float32 [512, 8], P(('dp', 'expert'))
- gate_grad: bfloat16 [32, 2048, 384], P(('dp', 'expert'))
- up_grad: bfloat16 [32, 2048, 384], P(('dp', 'expert'))
- down_grad: bfloat16 [32, 384, 2048], P(('dp', 'expert'))
Inputs may be any that keep to these rules, and one draw needn't show every extreme that they name: `expert_ids`: each row names 8 different experts. The rows of one device name no expert more than 16 times, and one expert is named exactly 16 times by the rows of every device.
All inputs are finite; a program needn't handle non-finite values.
Results may differ from a plain program's by a relative error of at most 0.0071.
Values may be sent and summed in bfloat16 or wider, within the bound.
A program may use at most 128 MiB of HBM per device.

v0:
```python
import jax
import jax.numpy as jnp
from jax import lax
from jax.sharding import PartitionSpec as P


def from_partner(shard, axis, apart):
    return lax.ppermute(shard, axis, [(i, i ^ 1 << apart) for i in range(lax.axis_size(axis))])


def contract(left_op, right_op, left_dim, right_dim):
    return lax.dot_general(
        left_op,
        right_op,
        (((left_dim,), (right_dim,)), ((), ())),
        preferred_element_type=jnp.float32,
    )


def deliver(buffer, dp_size, ex_size, experts, capacity, backward):
    feat_width = buffer.shape[1]
    doubled = jnp.broadcast_to(
        buffer.reshape(experts, 1, capacity, feat_width), (experts, 2, capacity, feat_width)
    )
    doubled = doubled.reshape(dp_size, ex_size, capacity, feat_width)
    if backward:
        arrived = lax.all_to_all(
            lax.all_to_all(doubled, "dp", split_axis=0, concat_axis=0, tiled=True),
            "expert",
            split_axis=1,
            concat_axis=1,
            tiled=True,
        )
    else:
        arrived = lax.all_to_all(
            lax.all_to_all(doubled, "dp", split_axis=0, concat_axis=0, tiled=True),
            "expert",
            split_axis=1,
            concat_axis=1,
            tiled=True,
        )
    return arrived.reshape(-1, feat_width)


def bring_back(partials_in, dp_size, ex_size, experts, capacity, half_index, backward):
    feat_width = partials_in.shape[1]
    if backward:
        partner = from_partner(partials_in, "expert", 0)
    else:
        partner = from_partner(partials_in, "expert", 0)
    summed = (partials_in.astype(jnp.float32) + partner.astype(jnp.float32)).astype(jnp.bfloat16)
    summed = summed.reshape(dp_size, ex_size, capacity, feat_width)
    own_half = lax.dynamic_slice_in_dim(summed, half_index * (capacity // 2), capacity // 2, 2)
    if backward:
        returned = lax.all_to_all(
            lax.all_to_all(own_half, "dp", split_axis=0, concat_axis=0, tiled=True),
            "expert",
            split_axis=1,
            concat_axis=1,
            tiled=True,
        )
    else:
        returned = lax.all_to_all(
            lax.all_to_all(own_half, "dp", split_axis=0, concat_axis=0, tiled=True),
            "expert",
            split_axis=1,
            concat_axis=1,
            tiled=True,
        )
    merged = returned.reshape(experts, capacity, feat_width)
    return merged.reshape(experts * capacity, feat_width)


def body(tokens, expert_ids, route_weight, out_grad, gate_weight, up_weight, down_weight):
    dp_size = lax.axis_size("dp")
    ex_size = lax.axis_size("expert")
    tok_count, feat_width = tokens.shape
    top_count = expert_ids.shape[1]
    experts = dp_size * ex_size // 2
    assigned = tok_count * top_count
    capacity = 2 * (assigned // experts)
    half_index = lax.axis_index("expert") % 2
    flat_ids = expert_ids.reshape(-1)
    onehot = (flat_ids[:, None] == jnp.arange(experts, dtype=jnp.int32)[None, :]).astype(jnp.int32)
    before = jnp.cumsum(onehot, axis=0) - onehot
    slot_ids = jnp.sum(before * onehot, axis=1)
    place_row = flat_ids * capacity + slot_ids
    source = (
        jnp.full((experts * capacity,), -1, jnp.int32)
        .at[place_row]
        .set(jnp.arange(assigned, dtype=jnp.int32))
    )
    filled = source >= 0
    assign = jnp.maximum(source, 0)
    rows_tok = assign // top_count
    send_rows = jnp.where(filled[:, None], tokens[rows_tok], jnp.zeros((), jnp.bfloat16))
    in_rows = deliver(send_rows, dp_size, ex_size, experts, capacity, False)
    w_gate = gate_weight[0]
    w_up = up_weight[0]
    w_down = down_weight[0]
    gate_act = jnp.dot(in_rows, w_gate, preferred_element_type=jnp.float32)
    up_act = jnp.dot(in_rows, w_up, preferred_element_type=jnp.float32)
    sig_gate = jax.nn.sigmoid(gate_act)
    hidden = (gate_act * sig_gate * up_act).astype(jnp.bfloat16)
    partial_value = jnp.dot(hidden, w_down, preferred_element_type=jnp.float32).astype(jnp.bfloat16)
    expert_table = bring_back(partial_value, dp_size, ex_size, experts, capacity, half_index, False)
    expert_rows = expert_table[place_row].reshape(tok_count, top_count, feat_width)
    layer_out = jnp.sum(route_weight[:, :, None] * expert_rows.astype(jnp.float32), axis=1).astype(
        jnp.bfloat16
    )
    route_grad = jnp.einsum("tkd,td->tk", expert_rows, out_grad, preferred_element_type=jnp.float32)
    scaled = (route_weight[:, :, None] * out_grad[:, None, :].astype(jnp.float32)).astype(
        jnp.bfloat16
    )
    scaled = scaled.reshape(assigned, feat_width)
    send_grad = jnp.where(filled[:, None], scaled[assign], jnp.zeros((), jnp.bfloat16))
    grad_rows = deliver(send_grad, dp_size, ex_size, experts, capacity, True)
    hidden_grad = contract(grad_rows, w_down, 1, 1)
    gate_pre = (hidden_grad * up_act * sig_gate * (1.0 + gate_act * (1.0 - sig_gate))).astype(
        jnp.bfloat16
    )
    up_pre = (hidden_grad * gate_act * sig_gate).astype(jnp.bfloat16)
    partial_grad = (contract(gate_pre, w_gate, 1, 1) + contract(up_pre, w_up, 1, 1)).astype(
        jnp.bfloat16
    )
    gate_grad = contract(in_rows, gate_pre, 0, 0).astype(jnp.bfloat16)
    up_grad = contract(in_rows, up_pre, 0, 0).astype(jnp.bfloat16)
    down_grad = contract(hidden, grad_rows, 0, 0).astype(jnp.bfloat16)
    grad_table = bring_back(partial_grad, dp_size, ex_size, experts, capacity, half_index, True)
    expert_grad = grad_table[place_row].reshape(tok_count, top_count, feat_width)
    token_grad = jnp.sum(expert_grad.astype(jnp.float32), axis=1).astype(jnp.bfloat16)
    return (layer_out, token_grad, route_grad, gate_grad[None], up_grad[None], down_grad[None])


def solution(mesh):
    in_specs = (
        P(("dp", "expert"), None),
        P(("dp", "expert"), None),
        P(("dp", "expert"), None),
        P(("dp", "expert"), None),
        P(("dp", "expert"), None, None),
        P(("dp", "expert"), None, None),
        P(("dp", "expert"), None, None),
    )
    out_specs = (
        P(("dp", "expert"), None),
        P(("dp", "expert"), None),
        P(("dp", "expert"), None),
        P(("dp", "expert"), None, None),
        P(("dp", "expert"), None, None),
        P(("dp", "expert"), None, None),
    )
    return jax.shard_map(body, mesh=mesh, in_specs=in_specs, out_specs=out_specs, check_vma=False)
```

profile of v0, /device:TPU:0, one launch (start us, length us, event | category | flops | bytes accessed | tf_op | source)
XLA Modules:
  0.0 294.7 jit_solution(16044852591126099703)
XLA Ops:
  7.3 2.3 gather_fusion
  11.3 55.4 %all_to_all.40 = bf16[8,4,16,2048]{3,2,1,0:T(8,128)(2,1)} all-to-all(bf16[8,4,16,2048]{3,2,1,0:T(8,128)(2,1)S(1)} %bitcast.69), channel_id=1, replica_groups=mesh['dp'=8,'expert'=4] {'dp'}, dimensions={0} | all-to-all | bytes 4194304 | tf_op jit(solution)/shard_map/all_to_all | solution.py:36
  66.8 1.6 broadcast_in_dim.62
  68.4 4.3 %all-to-all-start.4 = ((bf16[8,4,16,2048]{3,2,1,0:T(8,128)(2,1)}), bf16[8,4,16,2048]{3,2,1,0:T(8,128)(2,1)}, u32[]{:S(2)}, u32[]{:S(2)}) async-start(bf16[8,4,16,2048]{3,2,1,0:T(8,128)(2,1)} %bitcast.68), calls=%async_computation.4 | async-start | bytes 4194304 | tf_op jit(solution)/shard_map/all_to_all | solution.py:28
  72.7 3.1 %copy.44 = bf16[8,4,16,2048]{3,2,0,1:T(8,128)(2,1)} copy(bf16[8,4,16,2048]{3,2,1,0:T(8,128)(2,1)} %all_to_all.40) | data formatting | bytes 4194304 | tf_op jit(solution)/shard_map/all_to_all | solution.py:36
  75.9 44.2 %all-to-all-done.4 = bf16[8,4,16,2048]{3,2,1,0:T(8,128)(2,1)} async-done(((bf16[8,4,16,2048]{3,2,1,0:T(8,128)(2,1)}), bf16[8,4,16,2048]{3,2,1,0:T(8,128)(2,1)}, u32[]{:S(2)}, u32[]{:S(2)}) %all-to-all-start.4) | async-done | bytes 2097184 | tf_op jit(solution)/shard_map/all_to_all | solution.py:28
  120.1 4.4 %all-to-all-start.1 = ((bf16[8,4,16,2048]{3,2,0,1:T(8,128)(2,1)}), bf16[8,4,16,2048]{3,2,0,1:T(8,128)(2,1)}, u32[]{:S(2)}, u32[]{:S(2)}) async-start(bf16[8,4,16,2048]{3,2,0,1:T(8,128)(2,1)} %copy.44), calls=%async_computation.1 | async-start | bytes 4194304 | tf_op jit(solution)/shard_map/all_to_all | solution.py:35
  124.5 3.2 %copy.49 = bf16[8,4,16,2048]{3,2,0,1:T(8,128)(2,1)} copy(bf16[8,4,16,2048]{3,2,1,0:T(8,128)(2,1)} %all-to-all-done.4) | data formatting | bytes 4194304 | tf_op jit(solution)/shard_map/all_to_all | solution.py:28
  127.7 22.5 %all-to-all-done.1 = bf16[8,4,16,2048]{3,2,0,1:T(8,128)(2,1)} async-done(((bf16[8,4,16,2048]{3,2,0,1:T(8,128)(2,1)}), bf16[8,4,16,2048]{3,2,0,1:T(8,128)(2,1)}, u32[]{:S(2)}, u32[]{:S(2)}) %all-to-all-start.1) | async-done | bytes 2097184 | tf_op jit(solution)/shard_map/all_to_all | solution.py:35
  150.2 4.4 %all-to-all-start.5 = ((bf16[8,4,16,2048]{3,2,0,1:T(8,128)(2,1)}), bf16[8,4,16,2048]{3,2,0,1:T(8,128)(2,1)}, u32[]{:S(2)}, u32[]{:S(2)}) async-start(bf16[8,4,16,2048]{3,2,0,1:T(8,128)(2,1)} %copy.49), calls=%async_computation.5 | async-start | bytes 4194304 | tf_op jit(solution)/shard_map/all_to_all | solution.py:27
  154.7 1.8 copy.45
  156.7 2.1 fusion.7
  158.9 2.1 fusion.11
  161.0 19.4 %all-to-all-done.5 = bf16[8,4,16,2048]{3,2,0,1:T(8,128)(2,1)} async-done(((bf16[8,4,16,2048]{3,2,0,1:T(8,128)(2,1)}), bf16[8,4,16,2048]{3,2,0,1:T(8,128)(2,1)}, u32[]{:S(2)}, u32[]{:S(2)}) %all-to-all-start.5) | async-done | bytes 2097184 | tf_op jit(solution)/shard_map/all_to_all | solution.py:27
  180.4 1.8 copy.50
  182.4 1.5 multiply_convert_fusion
  184.0 2.6 convolution_convert_fusion
  188.0 2.7 add_convert_fusion.1
  191.2 3.0 %add_convert_fusion.2 = bf16[512,2048]{1,0:T(8,128)(2,1)S(1)} fusion(bf16[512,2048]{1,0:T(8,128)(2,1)} %collective-permute-done, bf16[512,2048]{1,0:T(8,128)(2,1)} %convolution_convert_fusion), kind=kLoop, calls=%fused_computation.7 | loop fusion | flops 4194304 | bytes 6291456 | tf_op jit(solution)/shard_map/convert_element_type | solution.py:51
  195.2 3.7 %all-to-all-start.2 = ((bf16[8,4,8,2048]{3,2,1,0:T(8,128)(2,1)}), bf16[8,4,8,2048]{3,2,1,0:T(8,128)(2,1)S(1)}, u32[]{:S(2)}, u32[]{:S(2)}) async-start(bf16[8,4,8,2048]{3,2,1,0:T(8,128)(2,1)} %constant_dynamic-slice_fusion), calls=%async_computation.2 | async-start | bytes 2097152 | tf_op jit(solution)/shard_map/all_to_all | solution.py:64
  199.0 3.0 %add_convert_fusion = bf16[512,2048]{1,0:T(8,128)(2,1)S(1)} fusion(bf16[512,2048]{1,0:T(8,128)(2,1)} %collective-permute-done.1, bf16[512,2048]{1,0:T(8,128)(2,1)} %add_convert_fusion.1), kind=kLoop, calls=%fused_computation.5 | loop fusion | flops 4194304 | bytes 6291456 | tf_op jit(solution)/shard_map/convert_element_type | solution.py:51
  203.1 21.9 %all-to-all-done.2 = bf16[8,4,8,2048]{3,2,1,0:T(8,128)(2,1)S(1)} async-done(((bf16[8,4,8,2048]{3,2,1,0:T(8,128)(2,1)}), bf16[8,4,8,2048]{3,2,1,0:T(8,128)(2,1)S(1)}, u32[]{:S(2)}, u32[]{:S(2)}) %all-to-all-start.2) | async-done | bytes 1048608 | tf_op jit(solution)/shard_map/all_to_all | solution.py:64
  225.0 4.3 %all-to-all-start.6 = ((bf16[8,4,8,2048]{3,2,1,0:T(8,128)(2,1)}), bf16[8,4,8,2048]{3,2,1,0:T(8,128)(2,1)}, u32[]{:S(2)}, u32[]{:S(2)}) async-start(bf16[8,4,8,2048]{3,2,1,0:T(8,128)(2,1)} %constant_dynamic-slice_fusion.1), calls=%async_computation.6 | async-start | bytes 2097152 | tf_op jit(solution)/shard_map/all_to_all | solution.py:56
  230.3 24.5 %all-to-all-done.6 = bf16[8,4,8,2048]{3,2,1,0:T(8,128)(2,1)} async-done(((bf16[8,4,8,2048]{3,2,1,0:T(8,128)(2,1)}), bf16[8,4,8,2048]{3,2,1,0:T(8,128)(2,1)}, u32[]{:S(2)}, u32[]{:S(2)}) %all-to-all-start.6) | async-done | bytes 1048608 | tf_op jit(solution)/shard_map/all_to_all | solution.py:56
  254.8 3.5 %all-to-all-start.3 = ((bf16[8,4,8,2048]{3,2,0,1:T(8,128)(2,1)}), bf16[8,4,8,2048]{3,2,0,1:T(8,128)(2,1)S(1)}, u32[]{:S(2)}, u32[]{:S(2)}) async-start(bf16[8,4,8,2048]{3,2,0,1:T(8,128)(2,1)} %copy.46), calls=%async_computation.3 | async-start | bytes 2097152 | tf_op jit(solution)/shard_map/all_to_all | solution.py:63
  258.4 4.0 %fusion.1 = bf16[1,2048,384]{2,1,0:T(8,128)(2,1)} fusion(bf16[512,2048]{1,0:T(8,128)(2,1)} %bitcast.76, bf16[512,384]{1,0:T(8,128)(2,1)S(1)} %copy-done.10), kind=kOutput, calls=%fused_computation.13 | convolution fusion | flops 806092800 | bytes 4063232 | tf_op jit(solution)/shard_map/dot_general | solution.py:12
  262.4 2.4 copy.51
  264.8 8.0 %all-to-all-done.3 = bf16[8,4,8,2048]{3,2,0,1:T(8,128)(2,1)S(1)} async-done(((bf16[8,4,8,2048]{3,2,0,1:T(8,128)(2,1)}), bf16[8,4,8,2048]{3,2,0,1:T(8,128)(2,1)S(1)}, u32[]{:S(2)}, u32[]{:S(2)}) %all-to-all-start.3) | async-done | bytes 1048608 | tf_op jit(solution)/shard_map/all_to_all | solution.py:63
  272.8 4.3 %all-to-all-start.7 = ((bf16[8,4,8,2048]{3,2,0,1:T(8,128)(2,1)}), bf16[8,4,8,2048]{3,2,0,1:T(8,128)(2,1)}, u32[]{:S(2)}, u32[]{:S(2)}) async-start(bf16[8,4,8,2048]{3,2,0,1:T(8,128)(2,1)} %copy.51), calls=%async_computation.7 | async-start | bytes 2097152 | tf_op jit(solution)/shard_map/all_to_all | solution.py:55
  277.0 3.9 %fusion.2 = bf16[1,384,2048]{2,1,0:T(8,128)(2,1)} fusion(bf16[512,384]{1,0:T(8,128)(2,1)S(1)} %copy-done.12, bf16[512,2048]{1,0:T(8,128)(2,1)} %bitcast.67), kind=kOutput, calls=%fused_computation.14 | convolution fusion | flops 806092800 | bytes 4063232 | tf_op jit(solution)/shard_map/dot_general | solution.py:12
  280.9 2.5 fusion
  287.8 3.7 %all-to-all-done.7 = bf16[8,4,8,2048]{3,2,0,1:T(8,128)(2,1)} async-done(((bf16[8,4,8,2048]{3,2,0,1:T(8,128)(2,1)}), bf16[8,4,8,2048]{3,2,0,1:T(8,128)(2,1)}, u32[]{:S(2)}, u32[]{:S(2)}) %all-to-all-start.7) | async-done | bytes 1048608 | tf_op jit(solution)/shard_map/all_to_all | solution.py:55
  (71 shorter events, 21.2 us)
Async XLA Ops:
  0.6 181.6 %copy-start = (bf16[1,384,2048]{2,1,0:T(8,128)(2,1)S(1)}, bf16[1,384,2048]{2,1,0:T(8,128)(2,1)}, u32[]{:S(2)}) copy-start(bf16[1,384,2048]{2,1,0:T(8,128)(2,1)} %param.13) | copy-start | bytes 4718596
  5.9 1.4 copy-start.1
  68.4 51.7 %all-to-all-start.4 = ((bf16[8,4,16,2048]{3,2,1,0:T(8,128)(2,1)}), bf16[8,4,16,2048]{3,2,1,0:T(8,128)(2,1)}, u32[]{:S(2)}, u32[]{:S(2)}) async-start(bf16[8,4,16,2048]{3,2,1,0:T(8,128)(2,1)} %bitcast.68), calls=%async_computation.4 | async-start | bytes 4194304 | tf_op jit(solution)/shard_map/all_to_all | solution.py:28
  120.1 30.2 %all-to-all-start.1 = ((bf16[8,4,16,2048]{3,2,0,1:T(8,128)(2,1)}), bf16[8,4,16,2048]{3,2,0,1:T(8,128)(2,1)}, u32[]{:S(2)}, u32[]{:S(2)}) async-start(bf16[8,4,16,2048]{3,2,0,1:T(8,128)(2,1)} %copy.44), calls=%async_computation.1 | async-start | bytes 4194304 | tf_op jit(solution)/shard_map/all_to_all | solution.py:35
  150.2 30.2 %all-to-all-start.5 = ((bf16[8,4,16,2048]{3,2,0,1:T(8,128)(2,1)}), bf16[8,4,16,2048]{3,2,0,1:T(8,128)(2,1)}, u32[]{:S(2)}, u32[]{:S(2)}) async-start(bf16[8,4,16,2048]{3,2,0,1:T(8,128)(2,1)} %copy.49), calls=%async_computation.5 | async-start | bytes 4194304 | tf_op jit(solution)/shard_map/all_to_all | solution.py:27
  154.7 2.0 copy-start.7
  156.5 2.3 copy-start.4
  156.7 2.1 copy-start.6
  180.4 1.9 copy-start.14
  180.4 2.0 copy-start.15
  182.3 1.7 copy-start.2
  183.9 2.6 copy-start.11
  183.9 3.9 %copy-start.9 = (bf16[512,384]{1,0:T(8,128)(2,1)}, bf16[512,384]{1,0:T(8,128)(2,1)S(1)}, u32[]{:S(2)}) copy-start(bf16[512,384]{1,0:T(8,128)(2,1)S(1)} %get-tuple-element.6) | copy-start | bytes 1179652
  186.6 4.6 %collective-permute-start = (bf16[512,2048]{1,0:T(8,128)(2,1)}, bf16[512,2048]{1,0:T(8,128)(2,1)}, u32[]{:S(2)}, u32[]{:S(2)}) collective-permute-start(bf16[512,2048]{1,0:T(8,128)(2,1)} %convolution_convert_fusion), channel_id=1, source_target_pairs={{0,1},{1,0},{2,3},{3,2},{4,5},{5,4},{6,7},{7,6},{8,9},{9,8},{10,11... | collective-permute-start | bytes 6291464 | tf_op jit(solution)/shard_map/ppermute | solution.py:8
  186.6 1.4 copy-start.8
  190.7 8.3 %collective-permute-start.1 = (bf16[512,2048]{1,0:T(8,128)(2,1)}, bf16[512,2048]{1,0:T(8,128)(2,1)}, u32[]{:S(2)}, u32[]{:S(2)}) collective-permute-start(bf16[512,2048]{1,0:T(8,128)(2,1)} %add_convert_fusion.1), channel_id=1, source_target_pairs={{0,1},{1,0},{2,3},{3,2},{4,5},{5,4},{6,7},{7,6},{8,9},{9,8},{10,11... | collective-permute-start | bytes 6291464 | tf_op jit(solution)/shard_map/ppermute | solution.py:8
  195.2 29.7 %all-to-all-start.2 = ((bf16[8,4,8,2048]{3,2,1,0:T(8,128)(2,1)}), bf16[8,4,8,2048]{3,2,1,0:T(8,128)(2,1)S(1)}, u32[]{:S(2)}, u32[]{:S(2)}) async-start(bf16[8,4,8,2048]{3,2,1,0:T(8,128)(2,1)} %constant_dynamic-slice_fusion), calls=%async_computation.2 | async-start | bytes 2097152 | tf_op jit(solution)/shard_map/all_to_all | solution.py:64
  225.0 29.8 %all-to-all-start.6 = ((bf16[8,4,8,2048]{3,2,1,0:T(8,128)(2,1)}), bf16[8,4,8,2048]{3,2,1,0:T(8,128)(2,1)}, u32[]{:S(2)}, u32[]{:S(2)}) async-start(bf16[8,4,8,2048]{3,2,1,0:T(8,128)(2,1)} %constant_dynamic-slice_fusion.1), calls=%async_computation.6 | async-start | bytes 2097152 | tf_op jit(solution)/shard_map/all_to_all | solution.py:56
  229.3 29.1 %copy-start.10 = (bf16[512,384]{1,0:T(8,128)(2,1)S(1)}, bf16[512,384]{1,0:T(8,128)(2,1)}, u32[]{:S(2)}) copy-start(bf16[512,384]{1,0:T(8,128)(2,1)} %copy-done.9) | copy-start | bytes 1179652
  254.8 17.9 %all-to-all-start.3 = ((bf16[8,4,8,2048]{3,2,0,1:T(8,128)(2,1)}), bf16[8,4,8,2048]{3,2,0,1:T(8,128)(2,1)S(1)}, u32[]{:S(2)}, u32[]{:S(2)}) async-start(bf16[8,4,8,2048]{3,2,0,1:T(8,128)(2,1)} %copy.46), calls=%async_computation.3 | async-start | bytes 2097152 | tf_op jit(solution)/shard_map/all_to_all | solution.py:63
  262.4 14.6 %copy-start.12 = (bf16[512,384]{1,0:T(8,128)(2,1)S(1)}, bf16[512,384]{1,0:T(8,128)(2,1)}, u32[]{:S(2)}) copy-start(bf16[512,384]{1,0:T(8,128)(2,1)} %copy-done.11) | copy-start | bytes 1179652
  272.8 8.2 %copy-start.3 = (bf16[8,4,8,2048]{3,2,0,1:T(8,128)(2,1)}, bf16[8,4,8,2048]{3,2,0,1:T(8,128)(2,1)S(1)}, u32[]{:S(2)}) copy-start(bf16[8,4,8,2048]{3,2,0,1:T(8,128)(2,1)S(1)} %all-to-all-done.3) | copy-start | bytes 3145732
  272.8 18.8 %all-to-all-start.7 = ((bf16[8,4,8,2048]{3,2,0,1:T(8,128)(2,1)}), bf16[8,4,8,2048]{3,2,0,1:T(8,128)(2,1)}, u32[]{:S(2)}, u32[]{:S(2)}) async-start(bf16[8,4,8,2048]{3,2,0,1:T(8,128)(2,1)} %copy.51), calls=%async_computation.7 | async-start | bytes 2097152 | tf_op jit(solution)/shard_map/all_to_all | solution.py:55
  277.0 3.9 %copy-start.5 = (bf16[8,4,16,2048]{3,2,1,0:T(8,128)(2,1)S(1)}, bf16[8,4,16,2048]{3,2,1,0:T(8,128)(2,1)}, u32[]{:S(2)}) copy-start(bf16[8,4,16,2048]{3,2,1,0:T(8,128)(2,1)} %copy-done.4) | copy-start | bytes 6291460
  284.7 1.0 copy-start.13
where the time goes:
time: 296 us; the launch traced here: 295 us
  waiting for transfers between devices  144 us (49%)
  blocking collectives  55.4 us (19%)
  local copies, waits for them, and re-layouts  29.6 us (10%)
  starting transfers between devices  29.5 us (10%)
  matrix products  23.2 us (8%)
  other arithmetic  11.8 us (4%)
    all_to_all x1, blocking collectives, deliver(): lax.all_to_all(doubled, 'dp', split_axis=0, concat_axis=0, tiled=True)  55.4 us
    all_to_all x2, waiting for transfers between devices, bring_back(): lax.all_to_all(own_half, 'dp', split_axis=0, concat_axis=0, tiled=True)  46.4 us
    all_to_all x1, waiting for transfers between devices, deliver(): lax.all_to_all(doubled, 'dp', split_axis=0, concat_axis=0, tiled=True)  44.2 us
    all_to_all x2, waiting for transfers between devices, deliver(): lax.all_to_all(lax.all_to_all(doubled, 'dp', split_axis=0, concat_axis=0,...  41.9 us
    dot_general x6, matrix products, contract(): lax.dot_general(left_op, right_op, (((left_dim,), (right_dim,)), ((), ())...  15.8 us
    all_to_all x2, waiting for transfers between devices, bring_back(): lax.all_to_all(lax.all_to_all(own_half, 'dp', split_axis=0, concat_axis=0...  11.7 us
    all_to_all x2, starting transfers between devices, deliver(): lax.all_to_all(lax.all_to_all(doubled, 'dp', split_axis=0, concat_axis=0,...  8.89 us
    all_to_all x2, starting transfers between devices, bring_back(): lax.all_to_all(own_half, 'dp', split_axis=0, concat_axis=0, tiled=True)  8.01 us
  transfers between devices with their start and end apart: 9, of which 7 were waited for; matrix products, arithmetic and copies ran while one was open for 14% of the time, Pallas kernels for 0%

commit v1 on v0

--- a/solution.py
+++ b/solution.py
@@ -2,6 +2,13 @@
 import jax.numpy as jnp
 from jax import lax
 from jax.sharding import PartitionSpec as P
+
+resolve_pools = lambda patch, dim_i, out_dim: jnp.concatenate(
+    jax.lax.all_to_all(
+        jnp.stack(jnp.split(patch, jax.lax.axis_size("expert"), axis=dim_i)), "expert", 0, 0
+    ),
+    out_dim,
+)
 
 
 def from_partner(shard, axis, apart):
@@ -24,12 +31,8 @@
     )
     doubled = doubled.reshape(dp_size, ex_size, capacity, feat_width)
     if backward:
-        arrived = lax.all_to_all(
-            lax.all_to_all(doubled, "dp", split_axis=0, concat_axis=0, tiled=True),
-            "expert",
-            split_axis=1,
-            concat_axis=1,
-            tiled=True,
+        arrived = resolve_pools(
+            lax.all_to_all(doubled, "dp", split_axis=0, concat_axis=0, tiled=True), 1, 1
         )
     else:
         arrived = lax.all_to_all(

time: 296 us -> 299 us (1.010)
  waiting for transfers between devices: 144 us -> 151 us
  matrix products: 23.2 us -> 19.4 us
    all_to_all x0 -> x1, waiting for transfers between devices: none -> 22.5 us  [jax.lax.all_to_all(jnp.stack(jnp.split(patch, jax.lax.axis_size('expert')...]
    all_to_all x2 -> x1, waiting for transfers between devices: 41.9 us -> 22.6 us  [deliver(): lax.all_to_all(lax.all_to_all(doubled, 'dp', split_axis=0, concat_axis=0,...]
    all_to_all x2 -> x1, starting transfers between devices: 8.89 us -> 4.45 us  [deliver(): lax.all_to_all(lax.all_to_all(doubled, 'dp', split_axis=0, concat_axis=0,...]
    all_to_all x0 -> x1, starting transfers between devices: none -> 4.44 us  [jax.lax.all_to_all(jnp.stack(jnp.split(patch, jax.lax.axis_size('expert')...]
    reshape x0 -> x1, local copies, waits for them, and re-layouts: none -> 3.17 us  [jnp.concatenate(jax.lax.all_to_all(jnp.stack(jnp.split(patch, jax.lax.axi...]
    all_to_all x2 -> x1, local copies, waits for them, and re-layouts: 6.33 us -> 3.19 us  [deliver(): lax.all_to_all(doubled, 'dp', split_axis=0, concat_axis=0, tiled=True)]
  transfers between devices with their start and end apart: 9 -> 9, of which waited for: 7 -> 8; matrix products, arithmetic and copies ran while one was open for 14% -> 12% of each run, Pallas kernels for 0% -> 0%
where the time goes in v1:
time: 299 us; the launch traced here: 298 us
  waiting for transfers between devices  151 us (51%)
  blocking collectives  55.4 us (19%)
  local copies, waits for them, and re-layouts  29.1 us (10%)
  starting transfers between devices  28.9 us (10%)
  matrix products  19.4 us (6%)
  other arithmetic  12.7 us (4%)
    all_to_all x1, blocking collectives, deliver(): lax.all_to_all(doubled, 'dp', split_axis=0, concat_axis=0, tiled=True)  55.4 us
    all_to_all x2, waiting for transfers between devices, bring_back(): lax.all_to_all(own_half, 'dp', split_axis=0, concat_axis=0, tiled=True)  47.6 us
    all_to_all x1, waiting for transfers between devices, deliver(): lax.all_to_all(doubled, 'dp', split_axis=0, concat_axis=0, tiled=True)  44 us
    all_to_all x1, waiting for transfers between devices, deliver(): lax.all_to_all(lax.all_to_all(doubled, 'dp', split_axis=0, concat_axis=0,...  22.6 us
    all_to_all x1, waiting for transfers between devices, jax.lax.all_to_all(jnp.stack(jnp.split(patch, jax.lax.axis_size('expert')...  22.5 us
    dot_general x6, matrix products, contract(): lax.dot_general(left_op, right_op, (((left_dim,), (right_dim,)), ((), ())...  13.9 us
    all_to_all x2, waiting for transfers between devices, bring_back(): lax.all_to_all(lax.all_to_all(own_half, 'dp', split_axis=0, concat_axis=0...  13.3 us
    all_to_all x2, starting transfers between devices, bring_back(): lax.all_to_all(lax.all_to_all(own_half, 'dp', split_axis=0, concat_axis=0...  7.78 us
  transfers between devices with their start and end apart: 9, of which 8 were waited for; matrix products, arithmetic and copies ran while one was open for 12% of the time, Pallas kernels for 0%

profile of v1, /device:TPU:0, one launch (start us, length us, event | category | flops | bytes accessed | tf_op | source)
XLA Modules:
  0.0 297.9 jit_solution(6119601263001688691)
XLA Ops:
  5.9 1.4 gather_fusion.2
  7.3 2.3 gather_fusion
  9.6 1.4 broadcast_select_fusion
  11.3 55.4 %all_to_all.40 = bf16[8,4,16,2048]{3,2,1,0:T(8,128)(2,1)} all-to-all(bf16[8,4,16,2048]{3,2,1,0:T(8,128)(2,1)S(1)} %bitcast.84), channel_id=1, replica_groups=mesh['dp'=8,'expert'=4] {'dp'}, dimensions={0} | all-to-all | bytes 4194304 | tf_op jit(solution)/shard_map/all_to_all | solution.py:35
  66.8 1.6 broadcast_in_dim.60
  68.3 4.3 %all-to-all-start = ((bf16[8,4,16,2048]{3,2,1,0:T(8,128)(2,1)}), bf16[8,4,16,2048]{3,2,1,0:T(8,128)(2,1)}, u32[]{:S(2)}, u32[]{:S(2)}) async-start(bf16[8,4,16,2048]{3,2,1,0:T(8,128)(2,1)} %bitcast.83), calls=%async_computation | async-start | bytes 4194304 | tf_op jit(solution)/shard_map/all_to_all | solution.py:39
  72.7 1.7 slice_bitcast_fusion.3
  74.3 1.6 pad_maximum_fusion
  76.0 44.0 %all-to-all-done = bf16[8,4,16,2048]{3,2,1,0:T(8,128)(2,1)} async-done(((bf16[8,4,16,2048]{3,2,1,0:T(8,128)(2,1)}), bf16[8,4,16,2048]{3,2,1,0:T(8,128)(2,1)}, u32[]{:S(2)}, u32[]{:S(2)}) %all-to-all-start) | async-done | bytes 2097184 | tf_op jit(solution)/shard_map/all_to_all | solution.py:39
  120.0 4.4 %all-to-all-start.5 = ((bf16[4,8,1,16,2048]{4,3,1,2,0:T(8,128)(2,1)}), bf16[4,8,1,16,2048]{4,3,1,2,0:T(8,128)(2,1)}, u32[]{:S(2)}, u32[]{:S(2)}) async-start(bf16[4,8,1,16,2048]{4,3,1,2,0:T(8,128)(2,1)} %pad_maximum_fusion), calls=%async_computation.5 | async-start | bytes 4194304 | tf_op jit(solution)/shard_map/all_to_all | solution.py:7
  124.4 3.2 %copy.64 = bf16[8,4,16,2048]{3,2,0,1:T(8,128)(2,1)} copy(bf16[8,4,16,2048]{3,2,1,0:T(8,128)(2,1)} %all-to-all-done) | data formatting | bytes 4194304 | tf_op jit(solution)/shard_map/all_to_all | solution.py:39
  127.6 22.5 %all-to-all-done.5 = bf16[4,8,1,16,2048]{4,3,1,2,0:T(8,128)(2,1)} async-done(((bf16[4,8,1,16,2048]{4,3,1,2,0:T(8,128)(2,1)}), bf16[4,8,1,16,2048]{4,3,1,2,0:T(8,128)(2,1)}, u32[]{:S(2)}, u32[]{:S(2)}) %all-to-all-start.5) | async-done | bytes 2097184 | tf_op jit(solution)/shard_map/all_to_all | solution.py:7
  150.2 4.4 %all-to-all-start.1 = ((bf16[8,4,16,2048]{3,2,0,1:T(8,128)(2,1)}), bf16[8,4,16,2048]{3,2,0,1:T(8,128)(2,1)}, u32[]{:S(2)}, u32[]{:S(2)}) async-start(bf16[8,4,16,2048]{3,2,0,1:T(8,128)(2,1)} %copy.64), calls=%async_computation.1 | async-start | bytes 4194304 | tf_op jit(solution)/shard_map/all_to_all | solution.py:38
  154.6 3.2 %copy.72 = bf16[8,4,1,16,2048]{4,3,1,0,2:T(8,128)(2,1)} copy(bf16[8,4,1,16,2048]{4,3,0,2,1:T(8,128)(2,1)} %bitcast.18) | data formatting | bytes 4194304 | tf_op jit(solution)/shard_map/reshape | solution.py:6
  157.8 22.6 %all-to-all-done.1 = bf16[8,4,16,2048]{3,2,0,1:T(8,128)(2,1)} async-done(((bf16[8,4,16,2048]{3,2,0,1:T(8,128)(2,1)}), bf16[8,4,16,2048]{3,2,0,1:T(8,128)(2,1)}, u32[]{:S(2)}, u32[]{:S(2)}) %all-to-all-start.1) | async-done | bytes 2097184 | tf_op jit(solution)/shard_map/all_to_all | solution.py:38
  180.4 1.7 copy.65
  185.9 1.5 multiply_convert_fusion
  187.4 2.6 convolution_convert_fusion
  194.5 3.0 %add_convert_fusion.2 = bf16[512,2048]{1,0:T(8,128)(2,1)S(1)} fusion(bf16[512,2048]{1,0:T(8,128)(2,1)} %collective-permute-done, bf16[512,2048]{1,0:T(8,128)(2,1)} %convolution_convert_fusion), kind=kLoop, calls=%fused_computation.7 | loop fusion | flops 4194304 | bytes 6291456 | tf_op jit(solution)/shard_map/convert_element_type | solution.py:54
  198.6 3.7 %all-to-all-start.2 = ((bf16[8,4,8,2048]{3,2,1,0:T(8,128)(2,1)}), bf16[8,4,8,2048]{3,2,1,0:T(8,128)(2,1)S(1)}, u32[]{:S(2)}, u32[]{:S(2)}) async-start(bf16[8,4,8,2048]{3,2,1,0:T(8,128)(2,1)} %constant_dynamic-slice_fusion), calls=%async_computation.2 | async-start | bytes 2097152 | tf_op jit(solution)/shard_map/all_to_all | solution.py:67
  202.3 2.4 add_convert_fusion
  205.7 22.7 %all-to-all-done.2 = bf16[8,4,8,2048]{3,2,1,0:T(8,128)(2,1)S(1)} async-done(((bf16[8,4,8,2048]{3,2,1,0:T(8,128)(2,1)}), bf16[8,4,8,2048]{3,2,1,0:T(8,128)(2,1)S(1)}, u32[]{:S(2)}, u32[]{:S(2)}) %all-to-all-start.2) | async-done | bytes 1048608 | tf_op jit(solution)/shard_map/all_to_all | solution.py:67
  228.4 3.6 %all-to-all-start.6 = ((bf16[8,4,8,2048]{3,2,1,0:T(8,128)(2,1)}), bf16[8,4,8,2048]{3,2,1,0:T(8,128)(2,1)S(1)}, u32[]{:S(2)}, u32[]{:S(2)}) async-start(bf16[8,4,8,2048]{3,2,1,0:T(8,128)(2,1)} %constant_dynamic-slice_fusion.1), calls=%async_computation.6 | async-start | bytes 2097152 | tf_op jit(solution)/shard_map/all_to_all | solution.py:59
  233.1 24.9 %all-to-all-done.6 = bf16[8,4,8,2048]{3,2,1,0:T(8,128)(2,1)S(1)} async-done(((bf16[8,4,8,2048]{3,2,1,0:T(8,128)(2,1)}), bf16[8,4,8,2048]{3,2,1,0:T(8,128)(2,1)S(1)}, u32[]{:S(2)}, u32[]{:S(2)}) %all-to-all-start.6) | async-done | bytes 1048608 | tf_op jit(solution)/shard_map/all_to_all | solution.py:59
  258.0 3.5 %all-to-all-start.3 = ((bf16[8,4,8,2048]{3,2,0,1:T(8,128)(2,1)}), bf16[8,4,8,2048]{3,2,0,1:T(8,128)(2,1)S(1)}, u32[]{:S(2)}, u32[]{:S(2)}) async-start(bf16[8,4,8,2048]{3,2,0,1:T(8,128)(2,1)} %copy.66), calls=%async_computation.3 | async-start | bytes 2097152 | tf_op jit(solution)/shard_map/all_to_all | solution.py:66
  261.5 4.0 %fusion.1 = bf16[1,2048,384]{2,1,0:T(8,128)(2,1)} fusion(bf16[512,2048]{1,0:T(8,128)(2,1)} %bitcast.91, bf16[512,384]{1,0:T(8,128)(2,1)S(1)} %copy-done.12), kind=kOutput, calls=%fused_computation.13 | convolution fusion | flops 806092800 | bytes 4063232 | tf_op jit(solution)/shard_map/dot_general | solution.py:19
  265.6 2.5 copy.73
  268.1 7.9 %all-to-all-done.3 = bf16[8,4,8,2048]{3,2,0,1:T(8,128)(2,1)S(1)} async-done(((bf16[8,4,8,2048]{3,2,0,1:T(8,128)(2,1)}), bf16[8,4,8,2048]{3,2,0,1:T(8,128)(2,1)S(1)}, u32[]{:S(2)}, u32[]{:S(2)}) %all-to-all-start.3) | async-done | bytes 1048608 | tf_op jit(solution)/shard_map/all_to_all | solution.py:66
  275.9 4.3 %all-to-all-start.7 = ((bf16[8,4,8,2048]{3,2,0,1:T(8,128)(2,1)}), bf16[8,4,8,2048]{3,2,0,1:T(8,128)(2,1)}, u32[]{:S(2)}, u32[]{:S(2)}) async-start(bf16[8,4,8,2048]{3,2,0,1:T(8,128)(2,1)} %copy.73), calls=%async_computation.7 | async-start | bytes 2097152 | tf_op jit(solution)/shard_map/all_to_all | solution.py:58
  280.2 3.3 %fusion.2 = bf16[1,384,2048]{2,1,0:T(8,128)(2,1)} fusion(bf16[512,384]{1,0:T(8,128)(2,1)} %copy-done.13, bf16[512,2048]{1,0:T(8,128)(2,1)S(1)} %bitcast.82), kind=kOutput, calls=%fused_computation.14 | convolution fusion | flops 806092800 | bytes 4063232 | tf_op jit(solution)/shard_map/dot_general | solution.py:19
  283.5 2.5 fusion
  289.2 5.5 %all-to-all-done.7 = bf16[8,4,8,2048]{3,2,0,1:T(8,128)(2,1)} async-done(((bf16[8,4,8,2048]{3,2,0,1:T(8,128)(2,1)}), bf16[8,4,8,2048]{3,2,0,1:T(8,128)(2,1)}, u32[]{:S(2)}, u32[]{:S(2)}) %all-to-all-start.7) | async-done | bytes 1048608 | tf_op jit(solution)/shard_map/all_to_all | solution.py:58
  (70 shorter events, 23.2 us)
Async XLA Ops:
  0.6 184.9 %copy-start = (bf16[1,384,2048]{2,1,0:T(8,128)(2,1)S(1)}, bf16[1,384,2048]{2,1,0:T(8,128)(2,1)}, u32[]{:S(2)}) copy-start(bf16[1,384,2048]{2,1,0:T(8,128)(2,1)} %param.13) | copy-start | bytes 4718596
  5.9 1.4 copy-start.2
  68.3 51.7 %all-to-all-start = ((bf16[8,4,16,2048]{3,2,1,0:T(8,128)(2,1)}), bf16[8,4,16,2048]{3,2,1,0:T(8,128)(2,1)}, u32[]{:S(2)}, u32[]{:S(2)}) async-start(bf16[8,4,16,2048]{3,2,1,0:T(8,128)(2,1)} %bitcast.83), calls=%async_computation | async-start | bytes 4194304 | tf_op jit(solution)/shard_map/all_to_all | solution.py:39
  120.0 30.2 %all-to-all-start.5 = ((bf16[4,8,1,16,2048]{4,3,1,2,0:T(8,128)(2,1)}), bf16[4,8,1,16,2048]{4,3,1,2,0:T(8,128)(2,1)}, u32[]{:S(2)}, u32[]{:S(2)}) async-start(bf16[4,8,1,16,2048]{4,3,1,2,0:T(8,128)(2,1)} %pad_maximum_fusion), calls=%async_computation.5 | async-start | bytes 4194304 | tf_op jit(solution)/shard_map/all_to_all | solution.py:7
  150.2 30.2 %all-to-all-start.1 = ((bf16[8,4,16,2048]{3,2,0,1:T(8,128)(2,1)}), bf16[8,4,16,2048]{3,2,0,1:T(8,128)(2,1)}, u32[]{:S(2)}, u32[]{:S(2)}) async-start(bf16[8,4,16,2048]{3,2,0,1:T(8,128)(2,1)} %copy.64), calls=%async_computation.1 | async-start | bytes 4194304 | tf_op jit(solution)/shard_map/all_to_all | solution.py:38
  157.8 24.3 %copy-start.9 = (bf16[1,2048,384]{2,1,0:T(8,128)(2,1)S(1)}, bf16[1,2048,384]{2,1,0:T(8,128)(2,1)}, u32[]{:S(2)}) copy-start(bf16[1,2048,384]{2,1,0:T(8,128)(2,1)} %param.12) | copy-start | bytes 4718596
  182.1 1.3 copy-start.6
  182.1 2.2 copy-start.8
  184.3 1.6 copy-start.3
  187.4 2.6 copy-start.13
  187.4 3.9 %copy-start.11 = (bf16[512,384]{1,0:T(8,128)(2,1)}, bf16[512,384]{1,0:T(8,128)(2,1)S(1)}, u32[]{:S(2)}) copy-start(bf16[512,384]{1,0:T(8,128)(2,1)S(1)} %get-tuple-element.10) | copy-start | bytes 1179652
  190.0 4.5 %collective-permute-start = (bf16[512,2048]{1,0:T(8,128)(2,1)}, bf16[512,2048]{1,0:T(8,128)(2,1)}, u32[]{:S(2)}, u32[]{:S(2)}) collective-permute-start(bf16[512,2048]{1,0:T(8,128)(2,1)} %convolution_convert_fusion), channel_id=1, source_target_pairs={{0,1},{1,0},{2,3},{3,2},{4,5},{5,4},{6,7},{7,6},{8,9},{9,8},{10,11... | collective-permute-start | bytes 6291464 | tf_op jit(solution)/shard_map/ppermute | solution.py:15
  190.0 1.4 copy-start.10
  192.7 9.6 %collective-permute-start.1 = (bf16[512,2048]{1,0:T(8,128)(2,1)S(1)}, bf16[512,2048]{1,0:T(8,128)(2,1)}, u32[]{:S(2)}, u32[]{:S(2)}) collective-permute-start(bf16[512,2048]{1,0:T(8,128)(2,1)S(1)} %add_convert_fusion.1), channel_id=1, source_target_pairs={{0,1},{1,0},{2,3},{3,2},{4,5},{5,4},{6,7},{7,6},{8,9},{9,8},{10,11... | collective-permute-start | bytes 6291464 | tf_op jit(solution)/shard_map/ppermute | solution.py:15
  198.6 29.8 %all-to-all-start.2 = ((bf16[8,4,8,2048]{3,2,1,0:T(8,128)(2,1)}), bf16[8,4,8,2048]{3,2,1,0:T(8,128)(2,1)S(1)}, u32[]{:S(2)}, u32[]{:S(2)}) async-start(bf16[8,4,8,2048]{3,2,1,0:T(8,128)(2,1)} %constant_dynamic-slice_fusion), calls=%async_computation.2 | async-start | bytes 2097152 | tf_op jit(solution)/shard_map/all_to_all | solution.py:67
  228.4 29.6 %all-to-all-start.6 = ((bf16[8,4,8,2048]{3,2,1,0:T(8,128)(2,1)}), bf16[8,4,8,2048]{3,2,1,0:T(8,128)(2,1)S(1)}, u32[]{:S(2)}, u32[]{:S(2)}) async-start(bf16[8,4,8,2048]{3,2,1,0:T(8,128)(2,1)} %constant_dynamic-slice_fusion.1), calls=%async_computation.6 | async-start | bytes 2097152 | tf_op jit(solution)/shard_map/all_to_all | solution.py:59
  232.0 29.5 %copy-start.12 = (bf16[512,384]{1,0:T(8,128)(2,1)S(1)}, bf16[512,384]{1,0:T(8,128)(2,1)}, u32[]{:S(2)}) copy-start(bf16[512,384]{1,0:T(8,128)(2,1)} %copy-done.11) | copy-start | bytes 1179652
  258.0 3.5 %copy-start.5 = (bf16[8,4,8,2048]{3,2,1,0:T(8,128)(2,1)}, bf16[8,4,8,2048]{3,2,1,0:T(8,128)(2,1)S(1)}, u32[]{:S(2)}) copy-start(bf16[8,4,8,2048]{3,2,1,0:T(8,128)(2,1)S(1)} %all-to-all-done.6) | copy-start | bytes 3145732
  258.0 17.9 %all-to-all-start.3 = ((bf16[8,4,8,2048]{3,2,0,1:T(8,128)(2,1)}), bf16[8,4,8,2048]{3,2,0,1:T(8,128)(2,1)S(1)}, u32[]{:S(2)}, u32[]{:S(2)}) async-start(bf16[8,4,8,2048]{3,2,0,1:T(8,128)(2,1)} %copy.66), calls=%async_computation.3 | async-start | bytes 2097152 | tf_op jit(solution)/shard_map/all_to_all | solution.py:66
  265.6 14.6 %copy-start.4 = (bf16[8,4,1,16,2048]{4,3,1,0,2:T(8,128)(2,1)S(1)}, bf16[8,4,1,16,2048]{4,3,1,0,2:T(8,128)(2,1)}, u32[]{:S(2)}) copy-start(bf16[8,4,1,16,2048]{4,3,1,0,2:T(8,128)(2,1)} %copy.72) | copy-start | bytes 6291460
  275.9 18.8 %all-to-all-start.7 = ((bf16[8,4,8,2048]{3,2,0,1:T(8,128)(2,1)}), bf16[8,4,8,2048]{3,2,0,1:T(8,128)(2,1)}, u32[]{:S(2)}, u32[]{:S(2)}) async-start(bf16[8,4,8,2048]{3,2,0,1:T(8,128)(2,1)} %copy.73), calls=%async_computation.7 | async-start | bytes 2097152 | tf_op jit(solution)/shard_map/all_to_all | solution.py:58
  280.2 3.3 %copy-start.7 = (bf16[8,4,16,2048]{3,2,1,0:T(8,128)(2,1)S(1)}, bf16[8,4,16,2048]{3,2,1,0:T(8,128)(2,1)}, u32[]{:S(2)}) copy-start(bf16[8,4,16,2048]{3,2,1,0:T(8,128)(2,1)} %copy-done.6) | copy-start | bytes 6291460
  286.0 1.0 copy-start.14
  296.0 1.9 copy-start.1
